TPU v7x, 32 devices: a whole 2x2x4 slice. The times are simulated.
32 devices in a mesh: row: 8 (over y, x, core), section: 4 (over z).
Axes of the slice: x: 2, y: 2, z: 4, core: 2. Of those that a mesh axis runs over, the one named last changes fastest.
Arguments:
- features: bfloat16 [8192, 256], P('row'), may hold values from -6 to 6
- weight: bfloat16 [256, 256], replicated, may hold values from -0.375 to 0.375
- cotangent: bfloat16 [8192, 256], P('row'), may hold values from -0.0625 to 0.0625
- counts: int32 [64, 16, 128, 128], P('row', 'section'), may hold values from 0 to 3, as said below
- columns: int32 [64, 16], P('row', 'section'), may hold values from 0 to 63, as said below
- live_slots: int32 [64, 4], P('row', 'section'), may hold values from 1 to 4, as said below
Outputs:
- output: bfloat16 [8192, 256], P('row')
- grad_weight: float32 [256, 256], replicated
Inputs may be any that keep to these rules, and one draw needn't show every extreme that they name: `columns`: every entry in a slot of section index s names a node block g with (g // 8) % 4 == s; the 4 slots of one row of blocks and one section index name distinct column blocks. Slots at k >= live_slots[b, s] are ignored; the value 4 occurs at every section index in every draw. `counts`: most entries are zero.
All inputs are finite; a program needn't handle non-finite values.
Results may differ from a plain program's by a relative error of at most 0.0055.
Values may be sent and summed in bfloat16 or wider, within the bound.
A program may use at most 64 MiB of HBM per device.

v0:
```python
import jax
import jax.numpy as jnp
from jax import lax
from jax.sharding import PartitionSpec as P


def per_device(features, weight, cotangent, counts, columns, live_slots):
    row_count = features.shape[0]
    feat_width = features.shape[1]
    block_count = columns.shape[0]
    slot_count = columns.shape[1]
    block_size = counts.shape[2]
    section_index = lax.axis_index("section")
    section_count = lax.axis_size("section")
    owner_count = lax.axis_size("row") // section_count
    everything = lax.all_gather(features, "row", axis=0, tiled=True)
    grouped = everything.reshape(owner_count, section_count, row_count, feat_width)
    window = lax.dynamic_index_in_dim(grouped, section_index, 1, keepdims=False)
    window = window.reshape(owner_count * block_count, block_size, feat_width)
    local_cols = columns // block_count // section_count * block_count + columns % block_count
    slot_used = jnp.arange(slot_count, dtype=jnp.int32)[None, :] < live_slots
    masked = jnp.where(slot_used[:, :, None, None], counts, 0)
    degree = jnp.sum(masked, axis=(1, 3)).astype(jnp.float32).reshape(row_count)
    edge_mats = masked.astype(jnp.bfloat16)
    picked = window[local_cols]
    partial_value = jnp.einsum(
        "rkij,rkjf->rif", edge_mats, picked, preferred_element_type=jnp.float32
    )
    partial_value = partial_value.reshape(row_count, feat_width)
    summed, degree_all = lax.psum((partial_value, degree), "section")
    aggregate = (summed * lax.rsqrt(1.0 + degree_all)[:, None]).astype(jnp.bfloat16)
    pre_act = jnp.dot(aggregate, weight, preferred_element_type=jnp.float32)
    gate_value = jax.nn.sigmoid(pre_act)
    output = (pre_act * gate_value).astype(jnp.bfloat16)
    grad_pre = (
        cotangent.astype(jnp.float32) * gate_value * (1.0 + pre_act * (1.0 - gate_value))
    ).astype(jnp.bfloat16)
    grad_local = lax.dot_general(
        aggregate, grad_pre, (((0,), (0,)), ((), ())), preferred_element_type=jnp.float32
    )
    grad_weight = lax.psum(grad_local, "row")
    return (output, grad_weight)


def solution(mesh):
    in_specs = (
        P("row", None),
        P(),
        P("row", None),
        P("row", "section", None, None),
        P("row", "section"),
        P("row", "section"),
    )
    out_specs = (P("row", None), P())
    return jax.shard_map(
        per_device, mesh=mesh, in_specs=in_specs, out_specs=out_specs, check_vma=False
    )
```

profile of v0, /device:TPU:0, one launch (start us, length us, event | category | flops | bytes accessed | tf_op | source)
XLA Modules:
  0.0 172.0 jit_solution(4953633193396426414)
XLA Ops:
  7.2 0.0 copy-start
  7.2 0.0 all-gather.2.cloned.1.call-start
  7.2 0.7 all-gather.2.cloned.1.call-update
  7.9 0.0 all-reduce.3.cloned.1.call-start
  8.0 0.7 compare_select_fusion
  8.7 0.1 copy.9
  8.8 0.1 reshape.45
  8.8 0.7 iota_compare_fusion
  9.6 39.8 %all-gather.2.cloned.1.call-done = bf16[8192,256]{1,0:T(8,128)(2,1)} async-done(((bf16[1024,256]{1,0:T(8,128)(2,1)}), bf16[8192,256]{1,0:T(8,128)(2,1)}) %all-gather.2.cloned.1.call-update) | async-done | bytes 4194320 | tf_op jit(solution)/shard_map/all_gather | solution.py:16
  49.4 1.3 constant_dynamic-slice_fusion
  50.6 0.7 gather_fusion
  51.3 3.2 %fusion = f32[8,128,256,1]{2,1,3,0:T(8,128)} fusion(bf16[8,4,128,256]{3,2,1,0:T(8,128)(2,1)S(1)} %bitcast.13, s32[8,4,128,128]{3,2,1,0:T(8,128)} %param.9, pred[8,4]{1,0:T(8,128)(4,1)S(1)} %iota_compare_fusion), kind=kOutput, calls=%fused_computation.3 | convolution fusion | flops 269484032 | bytes 5242912 | tf_op jit(solution)/shard_map/rkij,rkjf->rif/dot_general | solution.py:26
  54.5 0.0 all-reduce.3.cloned.1.call-update
  54.5 0.0 all-reduce.5.cloned.1.call-start
  54.6 1.9 %select_reduce_fusion = s32[8,128]{1,0:T(8,128)S(1)} fusion(s32[8,4,128,128]{3,2,1,0:T(8,128)} %param.9, pred[8,4]{1,0:T(8,128)(4,1)S(1)} %iota_compare_fusion), kind=kLoop, calls=%fused_computation.1 | loop fusion | flops 1047552 | bytes 2101280 | tf_op jit(solution)/shard_map/reduce_sum | solution.py:23
  56.5 11.9 %psum.22 = f32[1024]{0:T(1024)S(1)} all-reduce(f32[1024]{0:T(1024)S(1)} %convert_bitcast_fusion), channel_id=1, replica_groups=mesh['row'=8,'section'=4] {'section'}, use_global_device_ids=true, to_apply=%region_2.3 | all-reduce | flops 1024 | bytes 8192 | tf_op jit(solution)/shard_map/psum | solution.py:30
  68.5 0.0 copy-start.2
  68.5 38.2 %all-reduce.3.cloned.1.call-done = f32[1024,256]{1,0:T(8,128)} async-done(((f32[1024,256]{1,0:T(8,128)}), f32[1024,256]{1,0:T(8,128)}) %all-reduce.3.cloned.1.call-update) | async-done | bytes 1048592 | tf_op jit(solution)/shard_map/psum | solution.py:30
  106.6 0.0 copy-done
  106.6 0.0 copy-start.1
  106.6 2.6 %multiply_convert_fusion.1 = (bf16[1024,256]{1,0:T(8,128)(2,1)}, f32[1024,256]{1,0:T(8,128)S(1)}) fusion(bf16[256,256]{1,0:T(8,128)(2,1)S(1)} %copy-done, f32[1024,256]{1,0:T(8,128)} %all-reduce.3.cloned.1.call-done, f32[1024]{0:T(1024)S(1)} %add_rsqrt_fusion), kind=kOutput, calls=%fused_computation.5 | convolution fusion | flops 136052736 | bytes 2756608 | tf_op jit(solution)/shard_map/dot_general | solution.py:32
  109.2 0.0 copy-done.2
  109.2 0.0 copy-done.1
  109.2 1.5 fusion.3
  110.7 0.0 all-reduce.5.cloned.1.call-update
  110.7 53.1 %all-reduce.5.cloned.1.call-done = f32[256,256]{1,0:T(8,128)} async-done(((f32[256,256]{1,0:T(8,128)}), f32[256,256]{1,0:T(8,128)}) %all-reduce.5.cloned.1.call-update) | async-done | bytes 262160 | tf_op jit(solution)/shard_map/psum | solution.py:41
  163.8 1.7 copy.13
  (3 shorter events, 0.0 us)
Async XLA Ops:
  7.2 99.5 %copy-start = (bf16[256,256]{1,0:T(8,128)(2,1)S(1)}, bf16[256,256]{1,0:T(8,128)(2,1)}, u32[]{:S(2)}) copy-start(bf16[256,256]{1,0:T(8,128)(2,1)} %param.7) | copy-start | bytes 393220
  7.2 42.2 %all-gather.2.cloned.1.call-start = ((), (), s32[]{:S(2)}) async-start(), calls=%async_computation | async-start | bytes 4718592 | tf_op jit(solution)/shard_map/all_gather | solution.py:16
  7.9 98.7 %all-reduce.3.cloned.1.call-start = ((), (), s32[]{:S(2)}) async-start(), calls=%async_computation.1 | async-start | bytes 2097152 | tf_op jit(solution)/shard_map/psum | solution.py:30
  54.5 109.3 %all-reduce.5.cloned.1.call-start = ((), (), s32[]{:S(2)}) async-start(), calls=%async_computation.2 | async-start | bytes 524288 | tf_op jit(solution)/shard_map/psum | solution.py:41
  68.5 40.8 %copy-start.2 = (bf16[1024,256]{1,0:T(8,128)(2,1)S(1)}, bf16[1024,256]{1,0:T(8,128)(2,1)}, u32[]{:S(2)}) copy-start(bf16[1024,256]{1,0:T(8,128)(2,1)} %param.8) | copy-start | bytes 1572868
  106.6 2.6 %copy-start.1 = (f32[1024,256]{1,0:T(8,128)S(1)}, f32[1024,256]{1,0:T(8,128)}, u32[]{:S(2)}) copy-start(f32[1024,256]{1,0:T(8,128)} %all-reduce.3.cloned.1.call-done) | copy-start | bytes 3145732
Sparse Core Ops, SparseCore 0:
  9.9 39.4 all-gather.1
  54.7 51.9 all-reduce.2
  110.8 52.9 all-reduce.4
where the time goes:
time: 172 us
  waiting for transfers between devices  132 us (77%)
  between operations  13.8 us (8%)
  blocking collectives  11.9 us (7%)
  matrix products  7.25 us (4%)
  local copies, waits for them, and re-layouts  3.82 us (2%)
  other arithmetic  3.35 us (2%)
    psum x1, waiting for transfers between devices, per_device(): grad_weight = lax.psum(grad_local, 'row')  53.1 us
    all_gather x1, waiting for transfers between devices, per_device(): everything = lax.all_gather(features, 'row', axis=0, tiled=True)  39.8 us
    psum x1, waiting for transfers between devices, per_device(): summed, degree_all = lax.psum((partial_value, degree), 'section')  38.2 us
    psum x1, blocking collectives, per_device(): summed, degree_all = lax.psum((partial_value, degree), 'section')  11.9 us
  transfers between devices with their start and end apart: 3, of which 3 were waited for; matrix products, arithmetic and copies ran while one was open for 2% of the time, Pallas kernels for 0%

commit v1 on v0

--- a/solution.py
+++ b/solution.py
@@ -1,7 +1,26 @@
+import functools
 import jax
 import jax.numpy as jnp
 from jax import lax
 from jax.sharding import PartitionSpec as P
+
+
+def _supply_works(original, which_axis):
+    total_devices = lax.psum(1, axis_name=which_axis)
+
+    def create_signs(carry, y1):
+        if y1 >= total_devices:
+            return carry
+        a_next = range(total_devices)
+        block_last = map(lambda to_i: (to_i, to_i ^ y1), a_next)
+        right_arr = list(block_last)
+        state_next = lax.ppermute(carry, which_axis, perm=right_arr)
+        return create_signs(carry + state_next, 2 * y1)
+
+    return create_signs(original, 1)
+
+
+_match_quotas = functools.partial(_supply_works, which_axis="row")
 
 
 def per_device(features, weight, cotangent, counts, columns, live_slots):
@@ -38,7 +57,7 @@
     grad_local = lax.dot_general(
         aggregate, grad_pre, (((0,), (0,)), ((), ())), preferred_element_type=jnp.float32
     )
-    grad_weight = lax.psum(grad_local, "row")
+    grad_weight = _match_quotas(grad_local)
     return (output, grad_weight)
 
 

time: 172 us -> 136 us (0.79)
  waiting for transfers between devices: 132 us -> 93.1 us
  starting transfers between devices: 0.12 us -> 3.25 us
    psum x1 -> x0, waiting for transfers between devices: 53.1 us -> none  [per_device(): grad_weight = lax.psum(grad_local, 'row')]
    ppermute x0 -> x3, waiting for transfers between devices: none -> 14.4 us  [create_signs(): state_next = lax.ppermute(carry, which_axis, perm=right_arr)]
    ppermute x0 -> x3, starting transfers between devices: none -> 3.18 us  [create_signs(): state_next = lax.ppermute(carry, which_axis, perm=right_arr)]
  transfers between devices with their start and end apart: 3 -> 5, of which waited for: 3 -> 5; matrix products, arithmetic and copies ran while one was open for 2% -> 3% of each run, Pallas kernels for 0% -> 0%
where the time goes in v1:
time: 136 us; the launch traced here: 135 us
  waiting for transfers between devices  93.1 us (68%)
  between operations  14.1 us (10%)
  blocking collectives  12 us (9%)
  matrix products  6.52 us (5%)
  other arithmetic  4.15 us (3%)
  starting transfers between devices  3.25 us (2%)
  local copies, waits for them, and re-layouts  2.16 us (2%)
    all_gather x1, waiting for transfers between devices, per_device(): everything = lax.all_gather(features, 'row', axis=0, tiled=True)  39.8 us
    psum x1, waiting for transfers between devices, per_device(): summed, degree_all = lax.psum((partial_value, degree), 'section')  38.2 us
    ppermute x3, waiting for transfers between devices, create_signs(): state_next = lax.ppermute(carry, which_axis, perm=right_arr)  14.4 us
    psum x1, blocking collectives, per_device(): summed, degree_all = lax.psum((partial_value, degree), 'section')  12 us
    ppermute x3, starting transfers between devices, create_signs(): state_next = lax.ppermute(carry, which_axis, perm=right_arr)  3.18 us
    dot_general x1, matrix products, per_device(): jnp.einsum('rkij,rkjf->rif', edge_mats, picked, preferred_element_type=jn...  3.16 us
  transfers between devices with their start and end apart: 5, of which 5 were waited for; matrix products, arithmetic and copies ran while one was open for 3% of the time, Pallas kernels for 0%

profile of v1, /device:TPU:0, one launch (start us, length us, event | category | flops | bytes accessed | tf_op | source)
XLA Modules:
  0.0 135.2 jit_solution(17042718334168374081)
XLA Ops:
  7.2 0.0 copy-start
  7.2 0.0 all-gather.2.cloned.1.call-start
  7.2 0.7 all-gather.2.cloned.1.call-update
  7.9 0.0 all-reduce.2.cloned.1.call-start
  8.0 0.7 compare_select_fusion
  8.7 0.1 copy.9
  8.8 0.1 reshape.45
  8.8 0.7 iota_compare_fusion
  9.6 39.8 %all-gather.2.cloned.1.call-done = bf16[8192,256]{1,0:T(8,128)(2,1)} async-done(((bf16[1024,256]{1,0:T(8,128)(2,1)}), bf16[8192,256]{1,0:T(8,128)(2,1)}) %all-gather.2.cloned.1.call-update) | async-done | bytes 4194320 | tf_op jit(solution)/shard_map/all_gather | solution.py:35
  49.4 1.3 constant_dynamic-slice_fusion
  50.6 0.7 gather_fusion
  51.3 3.2 %fusion = f32[8,128,256,1]{2,1,3,0:T(8,128)} fusion(bf16[8,4,128,256]{3,2,1,0:T(8,128)(2,1)S(1)} %bitcast.13, s32[8,4,128,128]{3,2,1,0:T(8,128)} %param.9, pred[8,4]{1,0:T(8,128)(4,1)S(1)} %iota_compare_fusion), kind=kOutput, calls=%fused_computation.3 | convolution fusion | flops 269484032 | bytes 5242912 | tf_op jit(solution)/shard_map/rkij,rkjf->rif/dot_general | solution.py:45
  54.5 0.0 all-reduce.2.cloned.1.call-update
  54.5 1.9 %select_reduce_fusion = s32[8,128]{1,0:T(8,128)S(1)} fusion(s32[8,4,128,128]{3,2,1,0:T(8,128)} %param.9, pred[8,4]{1,0:T(8,128)(4,1)S(1)} %iota_compare_fusion), kind=kLoop, calls=%fused_computation.1 | loop fusion | flops 1047552 | bytes 2101280 | tf_op jit(solution)/shard_map/reduce_sum | solution.py:42
  56.4 12.0 %psum.15 = f32[1024]{0:T(1024)S(1)} all-reduce(f32[1024]{0:T(1024)S(1)} %convert_bitcast_fusion), channel_id=1, replica_groups=mesh['row'=8,'section'=4] {'section'}, use_global_device_ids=true, to_apply=%region_2.3 | all-reduce | flops 1024 | bytes 8192 | tf_op jit(solution)/shard_map/psum | solution.py:49
  68.5 0.0 copy-start.2
  68.5 38.2 %all-reduce.2.cloned.1.call-done = f32[1024,256]{1,0:T(8,128)} async-done(((f32[1024,256]{1,0:T(8,128)}), f32[1024,256]{1,0:T(8,128)}) %all-reduce.2.cloned.1.call-update) | async-done | bytes 1048592 | tf_op jit(solution)/shard_map/psum | solution.py:49
  106.6 0.0 copy-done
  106.6 0.0 copy-start.1
  106.6 2.6 %multiply_convert_fusion.1 = (bf16[1024,256]{1,0:T(8,128)(2,1)}, f32[1024,256]{1,0:T(8,128)S(1)}) fusion(bf16[256,256]{1,0:T(8,128)(2,1)S(1)} %copy-done, f32[1024,256]{1,0:T(8,128)} %all-reduce.2.cloned.1.call-done, f32[1024]{0:T(1024)S(1)} %add_rsqrt_fusion), kind=kOutput, calls=%fused_computation.5 | convolution fusion | flops 136052736 | bytes 2756608 | tf_op jit(solution)/shard_map/dot_general | solution.py:51
  109.2 0.0 copy-done.2
  109.2 0.0 copy-done.1
  109.2 0.7 fusion.3
  110.0 0.1 collective-permute-start
  110.1 1.5 %collective-permute-done = f32[256,256]{1,0:T(8,128)S(1)} collective-permute-done((f32[256,256]{1,0:T(8,128)S(1)}, f32[256,256]{1,0:T(8,128)S(1)}, u32[]{:S(2)}, u32[]{:S(2)}) %collective-permute-start) | collective-permute-done | bytes 262176 | tf_op jit(solution)/shard_map/ppermute | solution.py:17
  111.6 1.5 %collective-permute-start.1 = (f32[256,256]{1,0:T(8,128)S(1)}, f32[256,256]{1,0:T(8,128)S(1)}, u32[]{:S(2)}, u32[]{:S(2)}) collective-permute-start(f32[256,256]{1,0:T(8,128)S(1)} %add.55), channel_id=1, source_target_pairs={{0,8},{4,12},{8,0},{12,4},{16,24},{20,28},{24,16},{28,20},{1,9},{5... | collective-permute-start | bytes 786440 | tf_op jit(solution)/shard_map/ppermute | solution.py:17
  113.2 6.9 %collective-permute-done.1 = f32[256,256]{1,0:T(8,128)S(1)} collective-permute-done((f32[256,256]{1,0:T(8,128)S(1)}, f32[256,256]{1,0:T(8,128)S(1)}, u32[]{:S(2)}, u32[]{:S(2)}) %collective-permute-start.1) | collective-permute-done | bytes 262176 | tf_op jit(solution)/shard_map/ppermute | solution.py:17
  120.1 1.5 %collective-permute-start.2 = (f32[256,256]{1,0:T(8,128)S(1)}, f32[256,256]{1,0:T(8,128)S(1)}, u32[]{:S(2)}, u32[]{:S(2)}) collective-permute-start(f32[256,256]{1,0:T(8,128)S(1)} %add.56), channel_id=1, source_target_pairs={{0,16},{4,20},{8,24},{12,28},{16,0},{20,4},{24,8},{28,12},{1,17},{... | collective-permute-start | bytes 786440 | tf_op jit(solution)/shard_map/ppermute | solution.py:17
  121.6 6.0 %collective-permute-done.2 = f32[256,256]{1,0:T(8,128)S(1)} collective-permute-done((f32[256,256]{1,0:T(8,128)S(1)}, f32[256,256]{1,0:T(8,128)S(1)}, u32[]{:S(2)}, u32[]{:S(2)}) %collective-permute-start.2) | collective-permute-done | bytes 262176 | tf_op jit(solution)/shard_map/ppermute | solution.py:17
  127.7 0.7 add.57
  (5 shorter events, 0.1 us)
Async XLA Ops:
  7.2 99.4 %copy-start = (bf16[256,256]{1,0:T(8,128)(2,1)S(1)}, bf16[256,256]{1,0:T(8,128)(2,1)}, u32[]{:S(2)}) copy-start(bf16[256,256]{1,0:T(8,128)(2,1)} %param.7) | copy-start | bytes 393220
  7.2 42.2 %all-gather.2.cloned.1.call-start = ((), (), s32[]{:S(2)}) async-start(), calls=%async_computation | async-start | bytes 4718592 | tf_op jit(solution)/shard_map/all_gather | solution.py:35
  7.9 98.7 %all-reduce.2.cloned.1.call-start = ((), (), s32[]{:S(2)}) async-start(), calls=%async_computation.1 | async-start | bytes 2097152 | tf_op jit(solution)/shard_map/psum | solution.py:49
  68.5 40.8 %copy-start.2 = (bf16[1024,256]{1,0:T(8,128)(2,1)S(1)}, bf16[1024,256]{1,0:T(8,128)(2,1)}, u32[]{:S(2)}) copy-start(bf16[1024,256]{1,0:T(8,128)(2,1)} %param.8) | copy-start | bytes 1572868
  106.6 2.6 %copy-start.1 = (f32[1024,256]{1,0:T(8,128)S(1)}, f32[1024,256]{1,0:T(8,128)}, u32[]{:S(2)}) copy-start(f32[1024,256]{1,0:T(8,128)} %all-reduce.2.cloned.1.call-done) | copy-start | bytes 3145732
  110.0 1.6 %collective-permute-start = (f32[256,256]{1,0:T(8,128)S(1)}, f32[256,256]{1,0:T(8,128)S(1)}, u32[]{:S(2)}, u32[]{:S(2)}) collective-permute-start(f32[256,256]{1,0:T(8,128)S(1)} %fusion.3), channel_id=1, source_target_pairs={{0,4},{4,0},{8,12},{12,8},{16,20},{20,16},{24,28},{28,24},{1,5},{5... | collective-permute-start | bytes 786440 | tf_op jit(solution)/shard_map/ppermute | solution.py:17
  111.6 8.4 %collective-permute-start.1 = (f32[256,256]{1,0:T(8,128)S(1)}, f32[256,256]{1,0:T(8,128)S(1)}, u32[]{:S(2)}, u32[]{:S(2)}) collective-permute-start(f32[256,256]{1,0:T(8,128)S(1)} %add.55), channel_id=1, source_target_pairs={{0,8},{4,12},{8,0},{12,4},{16,24},{20,28},{24,16},{28,20},{1,9},{5... | collective-permute-start | bytes 786440 | tf_op jit(solution)/shard_map/ppermute | solution.py:17
  120.1 7.6 %collective-permute-start.2 = (f32[256,256]{1,0:T(8,128)S(1)}, f32[256,256]{1,0:T(8,128)S(1)}, u32[]{:S(2)}, u32[]{:S(2)}) collective-permute-start(f32[256,256]{1,0:T(8,128)S(1)} %add.56), channel_id=1, source_target_pairs={{0,16},{4,20},{8,24},{12,28},{16,0},{20,4},{24,8},{28,12},{1,17},{... | collective-permute-start | bytes 786440 | tf_op jit(solution)/shard_map/ppermute | solution.py:17
Sparse Core Ops, SparseCore 0:
  9.9 39.4 all-gather.1
  54.6 51.9 all-reduce.1
